TPU v7x, 32 devices: a whole 2x2x4 slice. The times are simulated.
32 devices in a mesh: dp: 4 (over z), krow: 8 (over y, x, core).
Axes of the slice: x: 2, y: 2, z: 4, core: 2. Of those that a mesh axis runs over, the one named last changes fastest.
Arguments:
- tokens: bfloat16 [12, 2048, 768], P('dp', 'krow'), may hold values from -6 to 6
- lengths: int32 [12], P('dp'), may hold values from 65 to 2048, as said below
- attn_gain: float32 [768], replicated, may hold values from 0.5 to 1.5
- attn_bias: float32 [768], replicated, may hold values from -1 to 1
- query_weight: bfloat16 [768, 768], replicated, may hold values from -0.4375 to 0.4375
- key_weight: bfloat16 [768, 768], replicated, may hold values from -0.21875 to 0.21875
- value_weight: bfloat16 [768, 768], replicated, may hold values from -0.21875 to 0.21875
- out_weight: bfloat16 [768, 768], replicated, may hold values from -3.5 to 3.5
- compress: bfloat16 [256, 2048], P('krow'), may hold values from -0.125 to 0.125
- ffn_gain: float32 [768], replicated, may hold values from 0.5 to 1.5
- ffn_bias: float32 [768], replicated, may hold values from -1 to 1
- up_weight: bfloat16 [768, 3072], replicated, may hold values from -0.21875 to 0.21875
- down_weight: bfloat16 [3072, 768], replicated, may hold values from -0.109375 to 0.109375
- cotangent: bfloat16 [12, 2048, 768], P('dp', 'krow'), may hold values from -6 to 6
Outputs:
- block_out: bfloat16 [12, 2048, 768], P('dp', 'krow')
- tokens_grad: bfloat16 [12, 2048, 768], P('dp', 'krow')
- attn_gain_grad: float32 [768], replicated
- attn_bias_grad: float32 [768], replicated
- query_weight_grad: float32 [768, 768], replicated
- key_weight_grad: float32 [768, 768], replicated
- value_weight_grad: float32 [768, 768], replicated
- out_weight_grad: float32 [768, 768], replicated
- compress_grad: float32 [256, 2048], P('krow')
- ffn_gain_grad: float32 [768], replicated
- ffn_bias_grad: float32 [768], replicated
- up_weight_grad: float32 [768, 3072], replicated
- down_weight_grad: float32 [3072, 768], replicated
- grad_norm: float32 [], replicated
Inputs may be any that keep to these rules, and one draw needn't show every extreme that they name: `lengths`: at least one sequence is 2048 positions long; positions at or past a sequence's length are padding.
All inputs are finite; a program needn't handle non-finite values.
Results may differ from a plain program's by a relative error of at most 0.019.
Values may be sent and summed in bfloat16 or wider, within the bound.
No kernel may reach another device: no remote copies, remote signals or barrier semaphores. Data moves between devices by JAX's collectives and lax.ppermute only.
A program may use at most 256 MiB of HBM per device.

v0:
```python
import jax
import jax.numpy as jnp
from jax import lax
from jax.sharding import PartitionSpec as P

D = 768
HEADS = 12
HEAD_DIM = 64
FF = 3072


EPSILON = 1e-05


def joined(value, axis, combine):
    everything = jax.tree.map(lambda part: lax.all_gather(part, axis), value)
    first = jax.tree.map(lambda part: part[0], everything)

    def hop(k, so_far):
        return combine(so_far, jax.tree.map(lambda part: part[k], everything))

    return lax.fori_loop(1, lax.axis_size(axis), hop, first)


def normalize(values, scale_vec, shift_vec):
    centred = values - jnp.mean(values, axis=-1, keepdims=True)
    spread = jnp.mean(centred * centred, axis=-1, keepdims=True)
    return centred * lax.rsqrt(spread + EPSILON) * scale_vec + shift_vec


def activate(hidden):
    return jax.nn.gelu(hidden, approximate=False)


def product(left_side, right_side):
    return jnp.dot(left_side, right_side, preferred_element_type=jnp.float32)


def product_back(grad_rows, weight):
    return lax.dot_general(
        grad_rows,
        weight,
        (((grad_rows.ndim - 1,), (1,)), ((), ())),
        preferred_element_type=jnp.float32,
    )


def contract_rows(left_side, right_side):
    left_flat = left_side.reshape(-1, left_side.shape[-1])
    right_flat = right_side.reshape(-1, right_side.shape[-1])
    return lax.dot_general(
        left_flat, right_flat, (((0,), (0,)), ((), ())), preferred_element_type=jnp.float32
    )


def combine_stats(left_pair, right_pair):
    largest = jnp.maximum(left_pair[0], right_pair[0])
    summed = left_pair[1] * jnp.exp(left_pair[0] - largest) + right_pair[1] * jnp.exp(
        right_pair[0] - largest
    )
    return (largest, summed)


def split_heads(matrix):
    return matrix.reshape(matrix.shape[0], matrix.shape[1], HEADS, HEAD_DIM)


def attend_scores(query_rows, key_rows):
    return jnp.einsum(
        "sthd,sjhd->shjt",
        split_heads(query_rows),
        split_heads(key_rows),
        preferred_element_type=jnp.float32,
    ) * HEAD_DIM ** (-0.5)


def mix_values(weights, value_rows):
    mixed_heads = jnp.einsum(
        "shjt,sjhd->sthd", weights, split_heads(value_rows), preferred_element_type=jnp.float32
    )
    return mixed_heads.reshape(mixed_heads.shape[0], mixed_heads.shape[1], D)


def head_sum(weights, rows):
    summed = jnp.einsum(
        "shjt,sthd->sjhd", weights, split_heads(rows), preferred_element_type=jnp.float32
    )
    return summed.reshape(summed.shape[0], summed.shape[1], D)


def prob_grads(grad_rows, value_rows):
    return jnp.einsum(
        "sthd,sjhd->shjt",
        split_heads(grad_rows),
        split_heads(value_rows),
        preferred_element_type=jnp.float32,
    )


def score_grads(attn_probs, grad_probs, row_dot):
    return (attn_probs * (grad_probs - row_dot[:, :, None, :])).astype(jnp.bfloat16)


def local(
    tokens,
    lengths,
    attn_gain,
    attn_bias,
    query_weight,
    key_weight,
    value_weight,
    out_weight,
    compress,
    ffn_gain,
    ffn_bias,
    up_weight,
    down_weight,
    cotangent,
):
    local_len = tokens.shape[1]
    full_len = local_len * lax.axis_size("krow")
    score_scale = HEAD_DIM ** (-0.5)
    positions = jnp.arange(full_len, dtype=jnp.int32)
    valid_mask = positions[None, :] < lengths[:, None]
    masked = compress[None, :, :] * valid_mask.astype(jnp.bfloat16)[:, None, :]
    inputs = tokens.astype(jnp.float32)
    normed, normed_back = jax.vjp(normalize, inputs, attn_gain, attn_bias)
    normed_low = normed.astype(jnp.bfloat16)
    queries = product(normed_low, query_weight).astype(jnp.bfloat16)
    full_normed, full_queries = (
        lax.all_gather(normed_low, "krow", axis=1, tiled=True),
        lax.all_gather(queries, "krow", axis=1, tiled=True),
    )
    summary = jnp.einsum(
        "sjt,std->sjd", masked, full_normed, preferred_element_type=jnp.float32
    ).astype(jnp.bfloat16)
    key_rows = product(summary, key_weight).astype(jnp.bfloat16)
    value_rows = product(summary, value_weight).astype(jnp.bfloat16)
    scores = attend_scores(full_queries, key_rows)
    local_top = jnp.max(scores, axis=2)
    local_sum = jnp.sum(jnp.exp(scores - local_top[:, :, None, :]), axis=2)
    largest, denominator = joined((local_top, local_sum), "krow", combine_stats)
    attn_probs = jnp.exp(scores - largest[:, :, None, :]) / denominator[:, :, None, :]
    mixed_rows = lax.psum_scatter(
        mix_values(attn_probs.astype(jnp.bfloat16), value_rows),
        "krow",
        scatter_dimension=1,
        tiled=True,
    )
    mixed_low = mixed_rows.astype(jnp.bfloat16)
    attended = inputs + product(mixed_low, out_weight)
    lifted, lifted_back = jax.vjp(normalize, attended, ffn_gain, ffn_bias)
    lifted_low = lifted.astype(jnp.bfloat16)
    active, active_back = jax.vjp(activate, product(lifted_low, up_weight))
    active_low = active.astype(jnp.bfloat16)
    block_out = (attended + product(active_low, down_weight)).astype(jnp.bfloat16)
    down_weight_grad = contract_rows(active_low, cotangent)
    (grad_hidden,) = active_back(product_back(cotangent, down_weight))
    grad_hidden = grad_hidden.astype(jnp.bfloat16)
    up_weight_grad = contract_rows(lifted_low, grad_hidden)
    lifted_input_grad, ffn_gain_grad, ffn_bias_grad = lifted_back(
        product_back(grad_hidden, up_weight)
    )
    grad_attended = cotangent.astype(jnp.float32) + lifted_input_grad
    grad_branch = grad_attended.astype(jnp.bfloat16)
    out_weight_grad = contract_rows(mixed_low, grad_branch)
    grad_mixed = product_back(grad_branch, out_weight).astype(jnp.bfloat16)
    full_grad_mixed = lax.all_gather(grad_mixed, "krow", axis=1, tiled=True)
    attn_probs = (
        jnp.exp(attend_scores(full_queries, key_rows) - largest[:, :, None, :])
        / denominator[:, :, None, :]
    )
    grad_probs = prob_grads(full_grad_mixed, value_rows)
    row_dot = lax.psum(jnp.sum(attn_probs * grad_probs, axis=2), "krow")
    grad_scores = score_grads(attn_probs, grad_probs, row_dot)
    grad_values = head_sum(attn_probs.astype(jnp.bfloat16), full_grad_mixed).astype(jnp.bfloat16)
    grad_keys = (head_sum(grad_scores, full_queries) * score_scale).astype(jnp.bfloat16)
    query_part = mix_values(grad_scores, key_rows) * score_scale
    grad_queries = lax.psum_scatter(
        query_part.astype(jnp.bfloat16), "krow", scatter_dimension=1, tiled=True
    )
    grad_summary = (
        product_back(grad_keys, key_weight) + product_back(grad_values, value_weight)
    ).astype(jnp.bfloat16)
    normed_part = jnp.einsum(
        "sjt,sjd->std", masked, grad_summary, preferred_element_type=jnp.float32
    )
    normed_extra = lax.psum_scatter(
        normed_part.astype(jnp.bfloat16), "krow", scatter_dimension=1, tiled=True
    ).astype(jnp.float32)
    compress_terms = jnp.einsum(
        "sjd,std->sjt", grad_summary, full_normed, preferred_element_type=jnp.float32
    )
    compress_local = jnp.sum(compress_terms * valid_mask.astype(jnp.float32)[:, None, :], axis=0)
    compress_grad = lax.psum(compress_local.astype(jnp.bfloat16), "dp").astype(jnp.float32)
    query_weight_grad = contract_rows(normed_low, grad_queries)
    key_weight_grad = contract_rows(summary, grad_keys)
    value_weight_grad = contract_rows(summary, grad_values)
    grad_normed = product_back(grad_queries, query_weight) + normed_extra
    normed_input_grad, attn_gain_grad, attn_bias_grad = normed_back(grad_normed)
    tokens_grad = (grad_attended + normed_input_grad).astype(jnp.bfloat16)
    norm_grads = jnp.stack([attn_gain_grad, attn_bias_grad, ffn_gain_grad, ffn_bias_grad])
    shards = (
        lax.psum_scatter(
            query_weight_grad.reshape(-1), ("dp", "krow"), scatter_dimension=0, tiled=True
        ),
        lax.psum_scatter(
            key_weight_grad.reshape(-1), ("dp", "krow"), scatter_dimension=0, tiled=True
        ),
        lax.psum_scatter(
            value_weight_grad.reshape(-1), ("dp", "krow"), scatter_dimension=0, tiled=True
        ),
        lax.psum_scatter(
            out_weight_grad.reshape(-1), ("dp", "krow"), scatter_dimension=0, tiled=True
        ),
        lax.psum_scatter(
            up_weight_grad.reshape(-1), ("dp", "krow"), scatter_dimension=0, tiled=True
        ),
        lax.psum_scatter(
            down_weight_grad.reshape(-1), ("dp", "krow"), scatter_dimension=0, tiled=True
        ),
        lax.psum_scatter(norm_grads.reshape(-1), ("dp", "krow"), scatter_dimension=0, tiled=True),
    )
    gathered = (
        lax.all_gather(shards[0].astype(jnp.bfloat16), ("dp", "krow"), axis=0, tiled=True).astype(
            jnp.float32
        ),
        lax.all_gather(shards[1].astype(jnp.bfloat16), ("dp", "krow"), axis=0, tiled=True).astype(
            jnp.float32
        ),
        lax.all_gather(shards[2].astype(jnp.bfloat16), ("dp", "krow"), axis=0, tiled=True).astype(
            jnp.float32
        ),
        lax.all_gather(shards[3].astype(jnp.bfloat16), ("dp", "krow"), axis=0, tiled=True).astype(
            jnp.float32
        ),
        lax.all_gather(shards[4].astype(jnp.bfloat16), ("dp", "krow"), axis=0, tiled=True).astype(
            jnp.float32
        ),
        lax.all_gather(shards[5].astype(jnp.bfloat16), ("dp", "krow"), axis=0, tiled=True).astype(
            jnp.float32
        ),
        lax.all_gather(shards[6].astype(jnp.bfloat16), ("dp", "krow"), axis=0, tiled=True).astype(
            jnp.float32
        ),
    )
    grad_norm = jnp.sqrt(sum((jnp.sum(member * member) for member in gathered)))
    norm_block = gathered[6].reshape(4, D)
    return (
        block_out,
        tokens_grad,
        norm_block[0],
        norm_block[1],
        gathered[0].reshape(D, D),
        gathered[1].reshape(D, D),
        gathered[2].reshape(D, D),
        gathered[3].reshape(D, D),
        compress_grad,
        norm_block[2],
        norm_block[3],
        gathered[4].reshape(D, FF),
        gathered[5].reshape(FF, D),
        grad_norm,
    )


def solution(mesh):
    in_specs = (
        P("dp", "krow", None),
        P("dp"),
        P(),
        P(),
        P(),
        P(),
        P(),
        P(),
        P("krow", None),
        P(),
        P(),
        P(),
        P(),
        P("dp", "krow", None),
    )
    out_specs = (
        P("dp", "krow", None),
        P("dp", "krow", None),
        P(),
        P(),
        P(),
        P(),
        P(),
        P(),
        P("krow", None),
        P(),
        P(),
        P(),
        P(),
        P(),
    )
    return jax.shard_map(local, mesh=mesh, in_specs=in_specs, out_specs=out_specs, check_vma=False)
```

profile of v0, /device:TPU:0, one launch (start us, length us, event | category | flops | bytes accessed | tf_op | source)
XLA Modules:
  0.0 1617.4 jit_solution(11979326768688022540)
XLA Ops:
  18.9 57.5 %all-gather.14.cloned.1.call-done = bf16[3,2048,768]{2,1,0:T(8,128)(2,1)} async-done(((bf16[3,256,768]{2,1,0:T(8,128)(2,1)}), bf16[3,2048,768]{2,1,0:T(8,128)(2,1)}) %all-gather.14.cloned.1.call-update) | async-done | bytes 9437200 | tf_op jit(solution)/shard_map/all_gather | solution.py:131
  76.4 5.5 convolution_convert_fusion.3
  82.5 55.2 %all-gather.16.cloned.1.call-done = bf16[3,2048,768]{2,1,0:T(8,128)(2,1)} async-done(((bf16[3,256,768]{2,1,0:T(8,128)(2,1)}), bf16[3,2048,768]{2,1,0:T(8,128)(2,1)}) %all-gather.16.cloned.1.call-update) | async-done | bytes 9437200 | tf_op jit(solution)/shard_map/all_gather | solution.py:132
  137.7 12.6 copy.54
  150.3 10.1 multiply_reduce_fusion.3
  160.6 6.7 exponential_reduce_fusion
  168.2 24.8 %all-gather.32.cloned.1.call-done = f32[24,12,2048]{2,1,0:T(8,128)} async-done(((f32[3,12,2048]{2,1,0:T(8,128)}), f32[24,12,2048]{2,1,0:T(8,128)}) %all-gather.32.cloned.1.call-update) | async-done | bytes 2359312 | tf_op jit(solution)/shard_map/all_gather | solution.py:16
  194.0 33.6 %all-gather.34.cloned.1.call-done = f32[24,12,2048]{2,1,0:T(8,128)} async-done(((f32[3,12,2048]{2,1,0:T(8,128)}), f32[24,12,2048]{2,1,0:T(8,128)}) %all-gather.34.cloned.1.call-update) | async-done | bytes 2359312 | tf_op jit(solution)/shard_map/all_gather | solution.py:16
  228.7 10.4 while.17
  239.0 12.8 fusion.28
  251.9 126.2 %reduce-scatter.4.cloned.1.call-done = f32[3,256,768]{1,2,0:T(8,128)} async-done(((f32[3,2048,768]{1,2,0:T(8,128)}), f32[3,256,768]{1,2,0:T(8,128)}) %reduce-scatter.4.cloned.1.call-update) | async-done | bytes 2359312 | tf_op jit(solution)/shard_map/reduce_scatter | solution.py:144
  381.5 9.1 fusion.31
  390.6 22.6 %multiply_convert_fusion.2 = (bf16[3,256,3072]{2,1,0:T(8,128)(2,1)}, f32[3,256,3072]{2,1,0:T(8,128)}) fusion(f32[3,256,3072]{2,1,0:T(8,128)S(1)} %get-tuple-element.190, u8[256,3072]{1,0:T(8,128)(4,1)S(1)} %get-tuple-element.150, u8[256,3072]{1,0:T(8,128)(4,1)S(1)} %get-tuple-element.149), kind=kLoop, calls=%fused_computation.18 | loop fusion | flops 165150720 | bytes 25165824 | tf_op jit(solution)/shard_map/convert_element_type | solution.py:155
  413.2 11.2 add_convert_fusion
  424.4 8.3 multiply_reduce_fusion.8
  438.6 58.9 %all-gather.18.cloned.1.call-done = bf16[3,2048,768]{2,1,0:T(8,128)(2,1)} async-done(((bf16[3,256,768]{2,1,0:T(8,128)(2,1)}), bf16[3,2048,768]{2,1,0:T(8,128)(2,1)}) %all-gather.18.cloned.1.call-update) | async-done | bytes 9437200 | tf_op jit(solution)/shard_map/all_gather | solution.py:168
  497.5 12.7 copy.58
  510.2 12.5 multiply_reduce_fusion.2
  522.8 54.2 %all-reduce.13.cloned.1.call-done = f32[3,12,2048]{2,1,0:T(8,128)} async-done(((f32[3,12,2048]{2,1,0:T(8,128)}), f32[3,12,2048]{2,1,0:T(8,128)}) %all-reduce.13.cloned.1.call-update) | async-done | bytes 294928 | tf_op jit(solution)/shard_map/psum | solution.py:174
  577.0 8.3 multiply_convert_fusion.1
  585.3 5.1 multiply_convert_fusion
  590.4 12.7 copy.61
  603.1 8.6 fusion.52
  612.2 10.2 fusion.58
  625.1 5.2 convolution_convert_fusion
  632.2 4.2 convolution_bitcast_fusion.2
  636.3 3.4 reshape.236
  639.8 7.5 convolution_bitcast_fusion.1
  647.3 5.9 copy.71
  653.2 6.4 convolution_bitcast_fusion
  659.7 10.7 reshape.240
  680.7 7.2 fusion.35
  688.0 71.6 %reduce-scatter.8.cloned.1.call-done = bf16[3,256,768]{2,1,0:T(8,128)(2,1)} async-done(((bf16[3,2048,768]{2,1,0:T(8,128)(2,1)}), bf16[3,256,768]{2,1,0:T(8,128)(2,1)}) %reduce-scatter.8.cloned.1.call-update) | async-done | bytes 1179664 | tf_op jit(solution)/shard_map/reduce_scatter | solution.py:188
  759.6 3.4 fusion.25
  772.5 456.3 %all-reduce.16 = (bf16[3072]{0:T(1024)(128)(2,1)S(1)}, bf16[589824]{0:T(1024)(128)(2,1)}, bf16[589824]{0:T(1024)(128)(2,1)}, bf16[589824]{0:T(1024)(128)(2,1)}, ...) all-reduce(f32[3072]{0:T(1024)S(1)} %reshape.229, ...), channel_id=7, replica_groups=mesh['dp'=4,'krow'=8] {'dp','krow'}, use_global_device_ids=true, to_apply=%region_21.0.clone | all-reduce | flops 7080960 | bytes 42485760
  1237.9 9.3 add_convert_fusion.2
  1249.1 39.1 %all-reduce = bf16[3072]{0:T(1024)(128)(2,1)S(1)} all-reduce(bf16[3072]{0:T(1024)(128)(2,1)S(1)} %dynamic-update-slice), channel_id=1, replica_groups=mesh['dp'=4,'krow'=8] {'dp','krow'}, use_global_device_ids=true, to_apply=%add | all-reduce | flops 3072 | bytes 12288
  1289.5 3.7 add_convert_fusion.1
  1295.7 42.8 %all-gather.22.cloned.1.call-done = bf16[589824]{0:T(1024)(128)(2,1)} async-done(((bf16[18432]{0:T(1024)(128)(2,1)}), bf16[589824]{0:T(1024)(128)(2,1)}) %all-gather.22.cloned.1.call-update) | async-done | bytes 1179664 | tf_op jit(solution)/shard_map/all_gather | solution.py:228
  1342.3 52.5 %all-gather.24.cloned.1.call-done = bf16[589824]{0:T(1024)(128)(2,1)} async-done(((bf16[18432]{0:T(1024)(128)(2,1)}), bf16[589824]{0:T(1024)(128)(2,1)}) %all-gather.24.cloned.1.call-update) | async-done | bytes 1179664 | tf_op jit(solution)/shard_map/all_gather | solution.py:231
  1397.9 53.6 %all-gather.26.cloned.1.call-done = bf16[589824]{0:T(1024)(128)(2,1)} async-done(((bf16[18432]{0:T(1024)(128)(2,1)}), bf16[589824]{0:T(1024)(128)(2,1)}) %all-gather.26.cloned.1.call-update) | async-done | bytes 1179664 | tf_op jit(solution)/shard_map/all_gather | solution.py:234
  1454.8 3.5 reshape.235
  1464.1 53.7 %all-gather.28.cloned.1.call-done = bf16[2359296]{0:T(1024)(128)(2,1)} async-done(((bf16[73728]{0:T(1024)(128)(2,1)}), bf16[2359296]{0:T(1024)(128)(2,1)}) %all-gather.28.cloned.1.call-update) | async-done | bytes 4718608 | tf_op jit(solution)/shard_map/all_gather | solution.py:237
  1517.9 5.0 multiply_reduce_fusion.1
  1523.6 60.5 %all-gather.30.cloned.1.call-done = bf16[2359296]{0:T(1024)(128)(2,1)} async-done(((bf16[73728]{0:T(1024)(128)(2,1)}), bf16[2359296]{0:T(1024)(128)(2,1)}) %all-gather.30.cloned.1.call-update) | async-done | bytes 4718608 | tf_op jit(solution)/shard_map/all_gather | solution.py:240
  1584.1 5.0 multiply_reduce_fusion
  1590.5 8.8 reshape.239
  1599.4 10.0 reshape.241
  (213 shorter events, 87.6 us)
Async XLA Ops:
  7.2 371.0 %copy-start = (bf16[768,768]{1,0:T(8,128)(2,1)S(1)}, bf16[768,768]{1,0:T(8,128)(2,1)}, u32[]{:S(2)}) copy-start(bf16[768,768]{1,0:T(8,128)(2,1)} %param.23) | copy-start | bytes 3538948
  7.2 7.6 copy-start.50
  7.2 69.2 %all-gather.14.cloned.1.call-start = ((), (), s32[]{:S(2)}) async-start(), calls=%async_computation.3 | async-start | bytes 10616832 | tf_op jit(solution)/shard_map/all_gather | solution.py:131
  11.9 64.5 %copy-start.9 = (bf16[32,2048]{1,0:T(8,128)(2,1)S(1)}, bf16[32,2048]{1,0:T(8,128)(2,1)}, u32[]{:S(2)}) copy-start(bf16[32,2048]{1,0:T(8,128)(2,1)} %param.24) | copy-start | bytes 393220
  14.7 123.0 %all-gather.16.cloned.1.call-start = ((), (), s32[]{:S(2)}) async-start(), calls=%async_computation.4 | async-start | bytes 10616832 | tf_op jit(solution)/shard_map/all_gather | solution.py:132
  18.2 174.8 %all-gather.32.cloned.1.call-start = ((), (), s32[]{:S(2)}) async-start(), calls=%async_computation.17 | async-start | bytes 3538944 | tf_op jit(solution)/shard_map/all_gather | solution.py:16
  81.9 85.7 %copy-start.7 = (bf16[3,32,768]{2,1,0:T(8,128)(2,1)}, bf16[3,32,768]{2,1,0:T(8,128)(2,1)S(1)}, u32[]{:S(2)}) copy-start(bf16[3,32,768]{2,1,0:T(8,128)(2,1)S(1)} %convolution_convert_fusion.3) | copy-start | bytes 442372
  82.5 67.9 %copy-start.19 = (bf16[3,32,12,64]{3,2,1,0:T(8,128)(2,1)}, bf16[3,32,12,64]{3,2,1,0:T(8,128)(2,1)S(1)}, u32[]{:S(2)}) copy-start(bf16[3,32,12,64]{3,2,1,0:T(8,128)(2,1)S(1)} %reshape.225) | copy-start | bytes 442372
  160.5 67.1 %all-gather.34.cloned.1.call-start = ((), (), s32[]{:S(2)}) async-start(), calls=%async_computation.18 | async-start | bytes 3538944 | tf_op jit(solution)/shard_map/all_gather | solution.py:16
  160.5 7.0 copy-start.17
  167.3 210.8 %reduce-scatter.4.cloned.1.call-start = ((), (), s32[]{:S(2)}) async-start(), calls=%async_computation.5 | async-start | bytes 21233664 | tf_op jit(solution)/shard_map/reduce_scatter | solution.py:144
  168.2 70.9 %copy-start.28 = (bf16[3,32,12,64]{3,2,1,0:T(8,128)(2,1)}, bf16[3,32,12,64]{3,2,1,0:T(8,128)(2,1)S(1)}, u32[]{:S(2)}) copy-start(bf16[3,32,12,64]{3,2,1,0:T(8,128)(2,1)S(1)} %reshape.224) | copy-start | bytes 442372
  251.8 126.3 %copy-start.3 = (bf16[3,256,768]{2,1,0:T(8,128)(2,1)S(1)}, bf16[3,256,768]{2,1,0:T(8,128)(2,1)}, u32[]{:S(2)}) copy-start(bf16[3,256,768]{2,1,0:T(8,128)(2,1)} %param.16) | copy-start | bytes 3538948
  251.9 129.6 %copy-start.30 = (f32[768]{0:T(1024)S(1)}, f32[768]{0:T(1024)}, u32[]{:S(2)}) copy-start(f32[768]{0:T(1024)} %param.25) | copy-start | bytes 9220
  251.9 129.6 %copy-start.31 = (f32[768]{0:T(1024)S(1)}, f32[768]{0:T(1024)}, u32[]{:S(2)}) copy-start(f32[768]{0:T(1024)} %param.26) | copy-start | bytes 9220
  251.9 245.6 %all-gather.18.cloned.1.call-start = ((), (), s32[]{:S(2)}) async-start(), calls=%async_computation.6 | async-start | bytes 10616832 | tf_op jit(solution)/shard_map/all_gather | solution.py:168
  381.1 51.7 %copy-start.4 = (f32[3,256,768]{2,1,0:T(8,128)}, f32[3,256,768]{2,1,0:T(8,128)S(1)}, u32[]{:S(2)}) copy-start(f32[3,256,768]{2,1,0:T(8,128)S(1)} %get-tuple-element.189) | copy-start | bytes 7077892
  390.6 22.6 %copy-start.10 = (bf16[3,256,768]{2,1,0:T(8,128)(2,1)S(1)}, bf16[3,256,768]{2,1,0:T(8,128)(2,1)}, u32[]{:S(2)}) copy-start(bf16[3,256,768]{2,1,0:T(8,128)(2,1)} %param.29) | copy-start | bytes 3538948
  438.5 71.7 %copy-start.29 = (bf16[3,32,12,64]{3,2,1,0:T(8,128)(2,1)S(1)}, bf16[3,32,12,64]{3,2,1,0:T(8,128)(2,1)}, u32[]{:S(2)}) copy-start(bf16[3,32,12,64]{3,2,1,0:T(8,128)(2,1)} %copy-done.28) | copy-start | bytes 442372
  438.5 138.5 %all-reduce.13.cloned.1.call-start = ((), (), s32[]{:S(2)}) async-start(), calls=%async_computation.7 | async-start | bytes 786432 | tf_op jit(solution)/shard_map/psum | solution.py:174
  522.7 165.3 %reduce-scatter.6.cloned.1.call-start = ((), (), s32[]{:S(2)}) async-start(), calls=%async_computation.8 | async-start | bytes 10616832 | tf_op jit(solution)/shard_map/reduce_scatter | solution.py:179
  577.0 8.3 copy-start.20
  603.1 156.5 %reduce-scatter.8.cloned.1.call-start = ((), (), s32[]{:S(2)}) async-start(), calls=%async_computation.9 | async-start | bytes 10616832 | tf_op jit(solution)/shard_map/reduce_scatter | solution.py:188
  612.2 11.1 copy-start.21
  612.2 10.6 copy-start.16
  622.8 7.5 copy-start.23
  630.3 616.8 %all-reduce.15.cloned.1.call-start = ((), (), s32[]{:S(2)}) async-start(), calls=%async_computation.14 | async-start | bytes 262144 | tf_op jit(solution)/shard_map/psum | solution.py:195
  639.8 13.5 slice-start
  659.7 10.7 copy-start.8
  659.7 10.7 copy-start.22
  680.7 79.0 %copy-start.33 = (f32[3,256]{1,0:T(4,128)S(1)}, f32[3,256]{1,0:T(4,128)}, u32[]{:S(2)}) copy-start(f32[3,256]{1,0:T(4,128)} %copy-done.32) | copy-start | bytes 9220
  680.7 79.0 %copy-start.38 = (f32[768]{0:T(1024)S(1)}, f32[768]{0:T(1024)}, u32[]{:S(2)}) copy-start(f32[768]{0:T(1024)} %param.18) | copy-start | bytes 9220
  687.9 75.1 %copy-start.37 = (f32[3,256]{1,0:T(4,128)S(1)}, f32[3,256]{1,0:T(4,128)}, u32[]{:S(2)}) copy-start(f32[3,256]{1,0:T(4,128)} %copy-done.36) | copy-start | bytes 9220
  687.9 76.5 %copy-start.35 = (f32[3,256]{1,0:T(4,128)S(1)}, f32[3,256]{1,0:T(4,128)}, u32[]{:S(2)}) copy-start(f32[3,256]{1,0:T(4,128)} %copy-done.34) | copy-start | bytes 9220
  688.0 78.7 %copy-start.18 = (bf16[3,256,768]{2,1,0:T(8,128)(2,1)S(1)}, bf16[3,256,768]{2,1,0:T(8,128)(2,1)}, u32[]{:S(2)}) copy-start(bf16[3,256,768]{2,1,0:T(8,128)(2,1)} %fusion.22) | copy-start | bytes 3538948
  688.0 605.2 %all-gather.20.cloned.1.call-start = ((), (), s32[]{:S(2)}) async-start(), calls=%async_computation.10 | async-start | bytes 1216512 | tf_op jit(solution)/shard_map/all_gather | solution.py:225
  759.6 7.0 copy-start.51
  1230.2 108.3 %all-gather.22.cloned.1.call-start = ((), (), s32[]{:S(2)}) async-start(), calls=%async_computation.11 | async-start | bytes 1216512 | tf_op jit(solution)/shard_map/all_gather | solution.py:228
  1231.6 163.2 %all-gather.24.cloned.1.call-start = ((), (), s32[]{:S(2)}) async-start(), calls=%async_computation.12 | async-start | bytes 1216512 | tf_op jit(solution)/shard_map/all_gather | solution.py:231
  1233.1 218.4 %all-gather.26.cloned.1.call-start = ((), (), s32[]{:S(2)}) async-start(), calls=%async_computation.13 | async-start | bytes 1216512 | tf_op jit(solution)/shard_map/all_gather | solution.py:234
  1234.5 283.3 %all-gather.28.cloned.1.call-start = ((), (), s32[]{:S(2)}) async-start(), calls=%async_computation.15 | async-start | bytes 4866048 | tf_op jit(solution)/shard_map/all_gather | solution.py:237
  1236.2 347.9 %all-gather.30.cloned.1.call-start = ((), (), s32[]{:S(2)}) async-start(), calls=%async_computation.16 | async-start | bytes 4866048 | tf_op jit(solution)/shard_map/all_gather | solution.py:240
  1237.9 51.0 %copy-start.44 = (f32[3,256]{1,0:T(4,128)S(1)}, f32[3,256]{1,0:T(4,128)}, u32[]{:S(2)}) copy-start(f32[3,256]{1,0:T(4,128)} %get-tuple-element.154) | copy-start | bytes 9220
  1237.9 51.6 %copy-start.40 = (f32[3,256]{1,0:T(4,128)S(1)}, f32[3,256]{1,0:T(4,128)}, u32[]{:S(2)}) copy-start(f32[3,256]{1,0:T(4,128)} %copy-done.39) | copy-start | bytes 9220
  1237.9 51.6 %copy-start.42 = (f32[3,256]{1,0:T(4,128)S(1)}, f32[3,256]{1,0:T(4,128)}, u32[]{:S(2)}) copy-start(f32[3,256]{1,0:T(4,128)} %copy-done.41) | copy-start | bytes 9220
  1342.3 117.9 %copy-start.13 = (bf16[589824]{0:T(1024)(128)(2,1)S(1)}, bf16[589824]{0:T(1024)(128)(2,1)}, u32[]{:S(2)}) copy-start(bf16[589824]{0:T(1024)(128)(2,1)} %all-gather.22.cloned.1.call-done) | copy-start | bytes 3538948
  1454.8 7.4 copy-start.12
  1590.5 18.8 %copy-start.1 = (bf16[768,768]{1,0:T(8,128)(2,1)S(1)}, bf16[768,768]{1,0:T(8,128)(2,1)}, u32[]{:S(2)}) copy-start(bf16[768,768]{1,0:T(8,128)(2,1)} %param.23) | copy-start | bytes 3538948
  (22 other events, 75.3 us)
Sparse Core Ops, SparseCore 0:
  14.8 61.5 all-gather.13
  78.9 58.8 all-gather.15
  160.6 32.3 all-gather.31
  195.3 32.3 all-gather.33
  252.0 126.1 reduce-scatter.3
  438.6 58.8 all-gather.17
  522.8 54.1 all-reduce.12
  603.2 75.7 reduce-scatter.5
  683.1 76.4 reduce-scatter.7
  762.4 34.4 all-reduce.14
  1230.3 51.9 all-gather.19
  1285.5 52.9 all-gather.21
  1341.8 52.9 all-gather.23
  1398.5 52.9 all-gather.25
  1455.3 62.5 all-gather.27
  1521.6 62.4 all-gather.29
where the time goes:
time: 1630 us; the launch traced here: 1620 us
  waiting for transfers between devices  746 us (46%)
  blocking collectives  495 us (30%)
  matrix products  154 us (9%)
  local copies, waits for them, and re-layouts  116 us (7%)
  other arithmetic  84.7 us (5%)
  between operations  20.8 us (1%)
    unnamed x2, blocking collectives  495 us
    reduce_scatter x1, waiting for transfers between devices, local(): lax.psum_scatter(mix_values(attn_probs.astype(jnp.bfloat16), value_rows),...  126 us
    reduce_scatter x1, waiting for transfers between devices, local(): lax.psum_scatter(normed_part.astype(jnp.bfloat16), 'krow', scatter_dimens...  71.6 us
    all_gather x1, waiting for transfers between devices, local(): lax.all_gather(shards[5].astype(jnp.bfloat16), ('dp', 'krow'), axis=0, ti...  60.5 us
    all_gather x1, waiting for transfers between devices, local(): full_grad_mixed = lax.all_gather(grad_mixed, 'krow', axis=1, tiled=True)  58.9 us
    all_gather x2, waiting for transfers between devices, joined(): everything = jax.tree.map(lambda part: lax.all_gather(part, axis), value)  58.4 us
    all_gather x1, waiting for transfers between devices, local(): lax.all_gather(normed_low, 'krow', axis=1, tiled=True)  57.5 us
    all_gather x1, waiting for transfers between devices, local(): lax.all_gather(queries, 'krow', axis=1, tiled=True)  55.2 us
  transfers between devices with their start and end apart: 16, of which 13 were waited for; matrix products, arithmetic and copies ran while one was open for 10% of the time, Pallas kernels for 0%

commit v1 on v0

v1 whole, which is shorter than its diff:
```python
import jax
import jax.numpy as jnp
from jax import lax
from jax.sharding import PartitionSpec as P

D = 768
HEADS = 12
HEAD_DIM = 64
FF = 3072
EPSILON = 1e-05
SCALE = HEAD_DIM ** (-0.5)
LOW = jnp.bfloat16


def swap(value, axis, mask):
    size = lax.axis_size(axis)
    return lax.ppermute(value, axis, [(i, i ^ mask) for i in range(size)])


def pick(value, at):
    return lax.dynamic_index_in_dim(value, at, 0, keepdims=False)


def bits_of(axis):
    return (lax.axis_size(axis) - 1).bit_length()


def bit(axis, at):
    return (lax.axis_index(axis) >> at) & 1


def in_order(mine, other, at):
    return jnp.where(at == 0, jnp.stack([mine, other]), jnp.stack([other, mine]))


def fold(value, axis, at):
    mine = bit(axis, at)
    return pick(value, mine) + swap(pick(value, 1 - mine), axis, 1 << at)


def unfold(value, axis, at):
    return in_order(value, swap(value, axis, 1 << at), bit(axis, at))


def sum_everywhere(part):
    count = bits_of("krow")
    rows, columns = part.shape
    half = fold(part.reshape(2, rows // 2, columns), "krow", 0)
    orders = [list(range(1, count)), list(range(count - 1, 0, -1))]
    pieces = []
    for color in range(2):
        piece = half.reshape(2, rows // 4, columns)[color]
        for at in orders[color]:
            piece = fold(piece.reshape(2, piece.shape[0] // 2, columns), "krow", at)
        pieces.append(piece)
    both = jnp.stack(pieces)
    for at in range(bits_of("dp")):
        both = both + swap(both, "dp", 1 << at)
    gathered = []
    for color in range(2):
        piece = both[color]
        for at in reversed(orders[color]):
            piece = unfold(piece, "krow", at).reshape(-1, columns)
        gathered.append(piece)
    half = jnp.stack(gathered).reshape(rows // 2, columns)
    return unfold(half, "krow", 0).reshape(rows, columns)


def sum_krow(part):
    size = lax.axis_size("krow")
    pairs = size // 2
    rows, columns = part.shape
    mine, place = bit("krow", 0), lax.axis_index("krow") >> 1
    parts = part.reshape(2, pairs, rows // size, columns)
    half = pick(parts, mine) + swap(pick(parts, 1 - mine).astype(LOW), "krow", 1).astype(
        jnp.float32
    )
    total = pick(half, place)
    for other in range(1, pairs):
        total = total + swap(pick(half, place ^ other).astype(LOW), "krow", 2 * other).astype(
            jnp.float32
        )
    total = total.astype(LOW)
    everyone = jnp.stack([total] + [swap(total, "krow", 2 * other) for other in range(1, pairs)])
    half = jnp.stack([pick(everyone, place ^ at) for at in range(pairs)])
    return unfold(half, "krow", 0).reshape(rows, columns)


def sum_small(value):
    for axis in ("krow", "dp"):
        for at in range(bits_of(axis)):
            value = value + swap(value, axis, 1 << at)
    return value


def normalize(values, scale_vec, shift_vec):
    centred = values - jnp.mean(values, axis=-1, keepdims=True)
    spread = jnp.mean(centred * centred, axis=-1, keepdims=True)
    return centred * lax.rsqrt(spread + EPSILON) * scale_vec + shift_vec


def activate(hidden):
    return jax.nn.gelu(hidden, approximate=False)


def product(left_side, right_side):
    return jnp.dot(left_side, right_side, preferred_element_type=jnp.float32)


def product_back(grad_rows, weight):
    return lax.dot_general(
        grad_rows,
        weight,
        (((grad_rows.ndim - 1,), (1,)), ((), ())),
        preferred_element_type=jnp.float32,
    )


def contract_rows(left_side, right_side):
    left_flat = left_side.reshape(-1, left_side.shape[-1])
    right_flat = right_side.reshape(-1, right_side.shape[-1])
    return lax.dot_general(
        left_flat, right_flat, (((0,), (0,)), ((), ())), preferred_element_type=jnp.float32
    ).astype(LOW)


def heads(matrix):
    return matrix.reshape(matrix.shape[0], matrix.shape[1], HEADS, HEAD_DIM)


def einsum(text, left_side, right_side):
    return jnp.einsum(text, left_side, right_side, preferred_element_type=jnp.float32)


def local(
    tokens,
    lengths,
    attn_gain,
    attn_bias,
    query_weight,
    key_weight,
    value_weight,
    out_weight,
    compress,
    ffn_gain,
    ffn_bias,
    up_weight,
    down_weight,
    cotangent,
):
    seqs, span, _ = tokens.shape
    ring = lax.axis_size("krow")
    rows = compress.shape[0] * ring
    columns = lax.all_to_all(
        compress.reshape(compress.shape[0], ring, span), "krow", 1, 0, tiled=False
    ).reshape(rows, span)
    positions = lax.axis_index("krow") * span + jnp.arange(span, dtype=jnp.int32)
    valid = positions[None, :] < lengths[:, None]
    masked = columns[None] * valid.astype(LOW)[:, None, :]
    inputs = tokens.astype(jnp.float32)
    normed, normed_back = jax.vjp(normalize, inputs, attn_gain, attn_bias)
    normed_low = normed.astype(LOW)
    summary_part = einsum("sjt,std->sjd", masked, normed_low)
    summary = sum_krow(summary_part.reshape(seqs * rows, D)).reshape(seqs, rows, D)
    queries = product(normed_low, query_weight).astype(LOW)
    key_rows = product(summary, key_weight).astype(LOW)
    value_rows = product(summary, value_weight).astype(LOW)
    scores = einsum("sthd,sjhd->shjt", heads(queries), heads(key_rows)) * SCALE
    attn_probs = jax.nn.softmax(scores, axis=2)
    probs_low = attn_probs.astype(LOW)
    mixed_low = einsum("shjt,sjhd->sthd", probs_low, heads(value_rows)).reshape(
        seqs, span, D
    ).astype(LOW)
    attended = inputs + product(mixed_low, out_weight)
    lifted, lifted_back = jax.vjp(normalize, attended, ffn_gain, ffn_bias)
    lifted_low = lifted.astype(LOW)
    active, active_back = jax.vjp(activate, product(lifted_low, up_weight))
    active_low = active.astype(LOW)
    block_out = (attended + product(active_low, down_weight)).astype(LOW)
    down_grad = sum_everywhere(contract_rows(active_low, cotangent))
    (grad_hidden,) = active_back(product_back(cotangent, down_weight))
    grad_hidden = grad_hidden.astype(LOW)
    up_grad = sum_everywhere(contract_rows(lifted_low, grad_hidden))
    lifted_input_grad, ffn_gain_grad, ffn_bias_grad = lifted_back(
        product_back(grad_hidden, up_weight)
    )
    grad_attended = cotangent.astype(jnp.float32) + lifted_input_grad
    grad_branch = grad_attended.astype(LOW)
    out_grad = contract_rows(mixed_low, grad_branch)
    grad_mixed = product_back(grad_branch, out_weight).astype(LOW)
    grad_probs = einsum("sthd,sjhd->shjt", heads(grad_mixed), heads(value_rows))
    row_dot = jnp.sum(attn_probs * grad_probs, axis=2, keepdims=True)
    grad_scores = (attn_probs * (grad_probs - row_dot)).astype(LOW)
    grad_values = einsum("shjt,sthd->sjhd", probs_low, heads(grad_mixed)).reshape(seqs, rows, D)
    grad_values = grad_values.astype(LOW)
    grad_keys = einsum("shjt,sthd->sjhd", grad_scores, heads(queries)) * SCALE
    grad_keys = grad_keys.reshape(seqs, rows, D).astype(LOW)
    grad_queries = einsum("shjt,sjhd->sthd", grad_scores, heads(key_rows)) * SCALE
    grad_queries = grad_queries.reshape(seqs, span, D).astype(LOW)
    grad_summary = product_back(grad_keys, key_weight) + product_back(grad_values, value_weight)
    grad_summary = sum_krow(grad_summary.reshape(seqs * rows, D)).reshape(seqs, rows, D)
    attn_grads = sum_everywhere(
        jnp.concatenate(
            [
                contract_rows(normed_low, grad_queries),
                contract_rows(summary, grad_keys),
                contract_rows(summary, grad_values),
                out_grad,
            ]
        )
    )
    compress_terms = einsum("sjd,std->sjt", grad_summary, normed_low)
    compress_part = jnp.sum(compress_terms * valid.astype(jnp.float32)[:, None, :], axis=0)
    compress_grad = lax.all_to_all(
        compress_part.astype(LOW).reshape(ring, rows // ring, span), "krow", 0, 1, tiled=False
    ).reshape(rows // ring, ring * span)
    for at in range(bits_of("dp")):
        compress_grad = compress_grad + swap(compress_grad, "dp", 1 << at)
    grad_normed = product_back(grad_queries, query_weight) + einsum(
        "sjt,sjd->std", masked, grad_summary
    )
    normed_input_grad, attn_gain_grad, attn_bias_grad = normed_back(grad_normed)
    tokens_grad = (grad_attended + normed_input_grad).astype(LOW)
    norms = sum_small(jnp.stack([attn_gain_grad, attn_bias_grad, ffn_gain_grad, ffn_bias_grad]))
    down_grad, up_grad, attn_grads = (
        g.astype(jnp.float32) for g in (down_grad, up_grad.reshape(D, FF), attn_grads)
    )
    grad_norm = jnp.sqrt(
        sum(jnp.sum(member * member) for member in (down_grad, up_grad, attn_grads, norms))
    )
    attn_grads = attn_grads.reshape(4, D, D)
    return (
        block_out,
        tokens_grad,
        norms[0],
        norms[1],
        attn_grads[0],
        attn_grads[1],
        attn_grads[2],
        attn_grads[3],
        compress_grad.astype(jnp.float32),
        norms[2],
        norms[3],
        up_grad,
        down_grad,
        grad_norm,
    )


def solution(mesh):
    rows, held = P("dp", "krow", None), P("krow", None)
    in_specs = (rows, P("dp"), P(), P(), P(), P(), P(), P(), held, P(), P(), P(), P(), rows)
    out_specs = (rows, rows, P(), P(), P(), P(), P(), P(), held, P(), P(), P(), P(), P())
    return jax.shard_map(local, mesh=mesh, in_specs=in_specs, out_specs=out_specs, check_vma=False)
```

time: 1630 us -> 508 us (0.31)
  waiting for transfers between devices: 746 us -> 201 us
  blocking collectives: 495 us -> 0 us
  local copies, waits for them, and re-layouts: 116 us -> 36.6 us
  starting transfers between devices: 0.84 us -> 61.9 us
  matrix products: 154 us -> 95.7 us
    unnamed x2 -> x0, blocking collectives: 495 us -> none
    all_gather x11 -> x0, waiting for transfers between devices: 493 us -> none  [the longest x1 60.5 us: local(): lax.all_gather(shards[5].astype(jnp.bfloat16), ('dp', 'krow'), axis=0, ti...]
    ppermute x0 -> x59, waiting for transfers between devices: none -> 198 us  [swap(): return lax.ppermute(value, axis, [(i, i ^ mask) for i in range(size)])]
    reduce_scatter x3 -> x0, waiting for transfers between devices: 198 us -> none  [the longest x1 126 us: local(): lax.psum_scatter(mix_values(attn_probs.astype(jnp.bfloat16), value_rows),...]
    psum x2 -> x0, waiting for transfers between devices: 54.2 us -> none  [the longest x1 54.2 us: local(): row_dot = lax.psum(jnp.sum(attn_probs * grad_probs, axis=2), 'krow')]
    reshape x14 -> x0, local copies, waits for them, and re-layouts: 52.5 us -> none  [the longest x1 10.7 us: local(): down_weight_grad.reshape(-1)]
    ppermute x0 -> x59, starting transfers between devices: none -> 52.5 us  [swap(): return lax.ppermute(value, axis, [(i, i ^ mask) for i in range(size)])]
    dot_general x9 -> x8, matrix products: 77.3 us -> 27 us  [einsum(): jnp.einsum(text, left_side, right_side, preferred_element_type=jnp.float32)]
  transfers between devices with their start and end apart: 16 -> 61, of which waited for: 13 -> 33; matrix products, arithmetic and copies ran while one was open for 10% -> 16% of each run, Pallas kernels for 0% -> 0%
where the time goes in v1:
time: 508 us; the launch traced here: 502 us
  waiting for transfers between devices  201 us (40%)
  other arithmetic  101 us (20%)
  matrix products  95.7 us (19%)
  starting transfers between devices  61.9 us (12%)
  local copies, waits for them, and re-layouts  36.6 us (7%)
  between operations  6.39 us (1%)
    ppermute x59, waiting for transfers between devices, swap(): return lax.ppermute(value, axis, [(i, i ^ mask) for i in range(size)])  198 us
    ppermute x59, starting transfers between devices, swap(): return lax.ppermute(value, axis, [(i, i ^ mask) for i in range(size)])  52.5 us
    dot_general x8, matrix products, einsum(): jnp.einsum(text, left_side, right_side, preferred_element_type=jnp.float32)  27 us
    dot_general x6, matrix products, product_back(): lax.dot_general(grad_rows, weight, (((grad_rows.ndim - 1,), (1,)), ((), (...  25 us
    convert_element_type x1, other arithmetic, local(): active_low = active.astype(LOW)  22.6 us
    dot_general x6, matrix products, product(): return jnp.dot(left_side, right_side, preferred_element_type=jnp.float32)  20.4 us
    reduce_sum x4, other arithmetic, local(): jnp.sum(member * member)  18.3 us
    convert_element_type x3, other arithmetic, local(): g.astype(jnp.float32)  17.1 us
  transfers between devices with their start and end apart: 61, of which 33 were waited for; matrix products, arithmetic and copies ran while one was open for 16% of the time, Pallas kernels for 0%

profile of v1, /device:TPU:0, one launch (start us, length us, event | category | flops | bytes accessed | tf_op | source)
XLA Modules:
  0.0 502.2 jit_solution(2410597405926707754)
XLA Ops:
  2.5 5.2 %all-to-all-start = ((bf16[1,32,8,256]{3,1,0,2:T(8,128)(2,1)}), bf16[1,32,8,256]{3,1,0,2:T(8,128)(2,1)S(1)}, u32[]{:S(2)}, u32[]{:S(2)}) async-start(bf16[1,32,8,256]{3,1,0,2:T(8,128)(2,1)} %copy.98), calls=%async_computation | async-start | bytes 262144 | tf_op jit(solution)/shard_map/all_to_all | solution.py:154
  10.3 2.8 all-to-all-done
  23.8 4.5 collective-permute-done.3
  34.6 3.9 collective-permute-done.6
  53.3 3.7 convolution_convert_fusion.4
  57.0 2.6 copy.102
  59.6 8.9 %fusion.110 = (f32[3,12,256]{2,1,0:T(8,128)}, f32[3,12,256,256]{3,2,1,0:T(8,128)}) fusion(bf16[3,256,12,64]{1,3,2,0:T(8,128)(2,1)} %bitcast.360, bf16[3,256,12,64]{1,3,2,0:T(8,128)(2,1)S(1)} %bitcast.346), kind=kOutput, calls=%fused_computation.248 | convolution fusion | flops 309068032 | bytes 11833344 | tf_op jit(solution)/shard_map/sub | solution.py:169
  68.4 4.9 fusion.42
  77.0 6.2 %fusion.39 = (u8[256,3072]{1,0:T(8,128)(4,1)S(1)}, u8[256,3072]{1,0:T(8,128)(4,1)S(1)}, f32[3,256,3072]{2,1,0:T(8,128)S(1)}) fusion(bf16[768,3072]{1,0:T(8,128)(2,1)S(1)} %bitcast.449, f32[3,256,768]{2,1,0:T(8,128)S(1)} %get-tuple-element.77, f32[768]{0:T(1024)S(1)} %copy-done.52, f32[768]{0:T(1024)S(1)} %copy-done.43, f32[3,256]{1,0:T(4,128)S(1)} %fusion.89, ...), kind=kOutput, calls=%fused_computation.90 | convolution fusion | flops 3655925760 | bytes 18100224 | tf_op jit(solution)/shard_map/dot_general | solution.py:107
  83.2 22.6 %multiply_convert_fusion.1 = (bf16[3,256,3072]{2,1,0:T(8,128)(2,1)}, f32[3,256,3072]{2,1,0:T(8,128)}) fusion(f32[3,256,3072]{2,1,0:T(8,128)S(1)} %get-tuple-element.78, u8[256,3072]{1,0:T(8,128)(4,1)S(1)} %get-tuple-element.15, u8[256,3072]{1,0:T(8,128)(4,1)S(1)} %get-tuple-element.14), kind=kLoop, calls=%fused_computation.16 | loop fusion | flops 165150720 | bytes 25165824 | tf_op jit(solution)/shard_map/convert_element_type | solution.py:178
  105.8 11.2 %add_convert_fusion = bf16[3,256,3072]{2,1,0:T(8,128)(2,1)} fusion(f32[3,256,3072]{2,1,0:T(8,128)} %get-tuple-element.31, f32[3,256,3072]{2,1,0:T(8,128)S(1)} %get-tuple-element.78, bf16[3,256,768]{2,1,0:T(8,128)(2,1)S(1)} %copy-done.11, bf16[3072,768]{1,0:T(8,128)(2,1)} %param.26), kind=kOutput, calls=%fused_computation.15 | convolution fusion | flops 3656908800 | bytes 29491200 | tf_op jit(solution)/shard_map/dot_general | solution.py:111
  117.0 8.3 %multiply_reduce_fusion.5 = (f32[768]{0:T(1024)}, f32[3,256]{1,0:T(4,128)S(1)}, f32[768]{0:T(1024)}, f32[3,256,768]{2,1,0:T(8,128)S(1)}) fusion(f32[3,256,768]{2,1,0:T(8,128)S(1)} %get-tuple-element.77, f32[3,256]{1,0:T(4,128)S(1)} %fusion.89, f32[3,256]{1,0:T(4,128)S(1)} %broadcast_multiply_fusion, f32[768]{0:T(1024)S(1)} %copy-done.43, ...), kind=kOutput, calls=%fused_computation.76 | convolution fusion | flops 3628594944 | bytes 14174208 | tf_op jit(solution)/shard_map/dot_general | solution.py:111
  133.2 8.4 %multiply_reduce_fusion.3 = (f32[3,12,256]{2,1,0:T(8,128)}, f32[3,12,256,256]{3,2,1,0:T(8,128)}) fusion(f32[3,12,256,256]{3,2,1,0:T(8,128)} %get-tuple-element.75, f32[3,12,256]{2,1,0:T(8,128)} %get-tuple-element.74, bf16[3,256,12,64]{1,3,2,0:T(8,128)(2,1)S(1)} %bitcast.419, bf16[3,256,12,64]{1,3,2,0:T(8,128)(2,1)} %bitcast.420), kind=kOutput, calls=%fused_computation.14 | convolution fusion | flops 309058560 | bytes 21307392 | tf_op jit(solution)/shard_map/sthd,sjhd->shjt/dot_general | solution.py:132
  141.7 11.2 %multiply_convert_fusion = bf16[3,12,256,256]{3,2,1,0:T(8,128)(2,1)} fusion(f32[3,12,256,256]{3,2,1,0:T(8,128)} %get-tuple-element.81, f32[3,12,256]{2,1,0:T(8,128)} %get-tuple-element.80, f32[3,12,256,256]{3,2,1,0:T(8,128)} %get-tuple-element.75, f32[3,12,256]{2,1,0:T(8,128)} %get-tuple-element.74), kind=kLoop, calls=%fused_computation.13 | loop fusion | flops 9437184 | bytes 23666688 | tf_op jit(solution)/shard_map/convert_element_type | solution.py:193
  152.9 3.4 multiply_convert_fusion.3
  158.2 5.4 %fusion.45 = bf16[3,12,64,256]{3,2,1,0:T(8,128)(2,1)S(1)} fusion(bf16[3,256,12,64]{1,3,2,0:T(8,128)(2,1)S(1)} %bitcast.421, f32[3,12,256,256]{3,2,1,0:T(8,128)} %get-tuple-element.75, f32[3,12,256]{2,1,0:T(8,128)S(1)} %copy-done.27), kind=kOutput, calls=%fused_computation.100 | convolution fusion | flops 307298304 | bytes 11833344 | tf_op jit(solution)/shard_map/shjt,sthd->sjhd/dot_general | solution.py:132
  165.4 5.2 %bitcast_convert_fusion.1 = bf16[768,3072]{1,0:T(8,128)(2,1)S(1)} fusion(bf16[3,256,3072]{2,1,0:T(8,128)(2,1)S(1)} %bitcast.455, f32[3,256,768]{2,1,0:T(8,128)S(1)} %copy-done.10, f32[768]{0:T(1024)S(1)} %copy-done.53, f32[768]{0:T(1024)S(1)} %copy-done.44, f32[3,256]{1,0:T(4,128)S(1)} %copy-done.40, f32[3,256]{1,0:T(4,128)S(1)} %broadcast_multiply_fusion), kind=kOutput, calls=%fused_computation.9 | convolution fusion | flops 3629187072 | bytes 11808768 | tf_op jit(solution)/shard_map/dot_general | solution.py:122
  170.6 4.9 add_convert_fusion.2
  190.7 3.0 collective-permute-done.11
  201.2 2.5 collective-permute-done.14
  206.2 4.2 bitcast_convert_fusion
  227.1 4.3 all-to-all-start.1
  231.4 2.6 collective-permute-start.20
  234.1 2.6 bitcast_add_fusion.2
  246.0 7.2 %collective-permute-done.24 = bf16[384,768]{1,0:T(8,128)(2,1)S(1)} collective-permute-done((bf16[384,768]{1,0:T(8,128)(2,1)S(1)}, bf16[384,768]{1,0:T(8,128)(2,1)S(1)}, u32[]{:S(2)}, u32[]{:S(2)}) %collective-permute-start.24) | collective-permute-done | bytes 589856 | tf_op jit(solution)/shard_map/ppermute | solution.py:17
  255.3 10.5 %collective-permute-done.38 = bf16[96,3072]{1,0:T(8,128)(2,1)S(1)} collective-permute-done((bf16[96,3072]{1,0:T(8,128)(2,1)S(1)}, bf16[96,3072]{1,0:T(8,128)(2,1)S(1)}, u32[]{:S(2)}, u32[]{:S(2)}) %collective-permute-start.38) | collective-permute-done | bytes 589856 | tf_op jit(solution)/shard_map/ppermute | solution.py:17
  270.3 8.2 %collective-permute-done.50 = bf16[384,768]{1,0:T(8,128)(2,1)S(1)} collective-permute-done((bf16[384,768]{1,0:T(8,128)(2,1)S(1)}, bf16[384,768]{1,0:T(8,128)(2,1)S(1)}, u32[]{:S(2)}, u32[]{:S(2)}) %collective-permute-start.50) | collective-permute-done | bytes 589856 | tf_op jit(solution)/shard_map/ppermute | solution.py:17
  284.2 4.2 collective-permute-done.25
  292.1 2.6 collective-permute-done.39
  299.2 18.1 %collective-permute-done.26 = bf16[2,192,768]{2,1,0:T(8,128)(2,1)S(1)} collective-permute-done((bf16[2,192,768]{2,1,0:T(8,128)(2,1)S(1)}, bf16[2,192,768]{2,1,0:T(8,128)(2,1)S(1)}, u32[]{:S(2)}, u32[]{:S(2)}) %collective-permute-start.26) | collective-permute-done | bytes 589856 | tf_op jit(solution)/shard_map/ppermute | solution.py:17
  317.4 20.7 %collective-permute-done.40 = bf16[2,48,3072]{2,1,0:T(8,128)(2,1)S(1)} collective-permute-done((bf16[2,48,3072]{2,1,0:T(8,128)(2,1)S(1)}, bf16[2,48,3072]{2,1,0:T(8,128)(2,1)S(1)}, u32[]{:S(2)}, u32[]{:S(2)}) %collective-permute-start.40) | collective-permute-done | bytes 589856 | tf_op jit(solution)/shard_map/ppermute | solution.py:17
  339.6 5.3 %collective-permute-done.52 = bf16[2,192,768]{2,1,0:T(8,128)(2,1)S(1)} collective-permute-done((bf16[2,192,768]{2,1,0:T(8,128)(2,1)S(1)}, bf16[2,192,768]{2,1,0:T(8,128)(2,1)S(1)}, u32[]{:S(2)}, u32[]{:S(2)}) %collective-permute-start.52) | collective-permute-done | bytes 589856 | tf_op jit(solution)/shard_map/ppermute | solution.py:17
  346.0 26.5 %collective-permute-done.27 = bf16[2,192,768]{2,1,0:T(8,128)(2,1)S(1)} collective-permute-done((bf16[2,192,768]{2,1,0:T(8,128)(2,1)S(1)}, bf16[2,192,768]{2,1,0:T(8,128)(2,1)S(1)}, u32[]{:S(2)}, u32[]{:S(2)}) %collective-permute-start.27) | collective-permute-done | bytes 589856 | tf_op jit(solution)/shard_map/ppermute | solution.py:17
  374.5 10.6 %collective-permute-done.41 = bf16[2,48,3072]{2,1,0:T(8,128)(2,1)S(1)} collective-permute-done((bf16[2,48,3072]{2,1,0:T(8,128)(2,1)S(1)}, bf16[2,48,3072]{2,1,0:T(8,128)(2,1)S(1)}, u32[]{:S(2)}, u32[]{:S(2)}) %collective-permute-start.41) | collective-permute-done | bytes 589856 | tf_op jit(solution)/shard_map/ppermute | solution.py:17
  386.3 5.2 %collective-permute-done.53 = bf16[2,192,768]{2,1,0:T(8,128)(2,1)S(1)} collective-permute-done((bf16[2,192,768]{2,1,0:T(8,128)(2,1)S(1)}, bf16[2,192,768]{2,1,0:T(8,128)(2,1)S(1)}, u32[]{:S(2)}, u32[]{:S(2)}) %collective-permute-start.53) | collective-permute-done | bytes 589856 | tf_op jit(solution)/shard_map/ppermute | solution.py:17
  391.7 2.7 collective-permute-done.44
  394.5 4.1 collective-permute-done.56
  398.8 5.6 %collective-permute-done.54 = bf16[192,768]{1,0:T(8,128)(2,1)S(1)} collective-permute-done((bf16[192,768]{1,0:T(8,128)(2,1)S(1)}, bf16[192,768]{1,0:T(8,128)(2,1)S(1)}, u32[]{:S(2)}, u32[]{:S(2)}) %collective-permute-start.54) | collective-permute-done | bytes 294944 | tf_op jit(solution)/shard_map/ppermute | solution.py:17
  407.1 22.5 %collective-permute-done.57 = bf16[384,768]{1,0:T(8,128)(2,1)S(1)} collective-permute-done((bf16[384,768]{1,0:T(8,128)(2,1)S(1)}, bf16[384,768]{1,0:T(8,128)(2,1)S(1)}, u32[]{:S(2)}, u32[]{:S(2)}) %collective-permute-start.57) | collective-permute-done | bytes 589856 | tf_op jit(solution)/shard_map/ppermute | solution.py:17
  432.2 7.6 %collective-permute-done.43 = bf16[96,3072]{1,0:T(8,128)(2,1)S(1)} collective-permute-done((bf16[96,3072]{1,0:T(8,128)(2,1)S(1)}, bf16[96,3072]{1,0:T(8,128)(2,1)S(1)}, u32[]{:S(2)}, u32[]{:S(2)}) %collective-permute-start.43) | collective-permute-done | bytes 589856 | tf_op jit(solution)/shard_map/ppermute | solution.py:17
  448.2 3.0 collective-permute-done.33
  452.8 4.9 collective-permute-done.29
  460.2 6.8 %multiply_reduce_fusion.2 = f32[]{:T(128)} fusion(bf16[1,1536,768]{2,1,0:T(8,128)(2,1)} %bitcast.155, bf16[1,1536,768]{2,1,0:T(8,128)(2,1)} %bitcast.157, pred[]{:T(512)S(6)} %eq.6), kind=kLoop, calls=%fused_computation.12 | loop fusion | flops 14155775 | bytes 4718597 | tf_op jit(solution)/shard_map/reduce_sum | solution.py:229
  467.0 7.1 %multiply_reduce_fusion.1 = f32[]{:T(128)} fusion(bf16[1,384,3072]{2,1,0:T(8,128)(2,1)} %bitcast.121, bf16[1,384,3072]{2,1,0:T(8,128)(2,1)} %bitcast.123, pred[]{:T(512)S(6)} %eq.6), kind=kLoop, calls=%fused_computation.11 | loop fusion | flops 14155775 | bytes 4718597 | tf_op jit(solution)/shard_map/reduce_sum | solution.py:229
  474.1 8.0 %fusion.13 = f32[2,384,3072]{2,1,0:T(8,128)} fusion(bf16[1,384,3072]{2,1,0:T(8,128)(2,1)} %bitcast.123, bf16[1,384,3072]{2,1,0:T(8,128)(2,1)} %bitcast.121, pred[]{:T(512)S(6)} %eq.6), kind=kLoop, calls=%fused_computation.37 | loop fusion | flops 9437184 | bytes 14155777 | tf_op jit(solution)/shard_map/convert_element_type | solution.py:226
  482.1 8.2 %fusion.14 = f32[2,1536,768]{2,1,0:T(8,128)} fusion(bf16[1,1536,768]{2,1,0:T(8,128)(2,1)} %bitcast.157, bf16[1,1536,768]{2,1,0:T(8,128)(2,1)} %bitcast.155, pred[]{:T(512)S(6)} %eq.6), kind=kLoop, calls=%fused_computation.39 | loop fusion | flops 9437184 | bytes 14155777 | tf_op jit(solution)/shard_map/convert_element_type | solution.py:226
  491.2 3.1 multiply_reduce_fusion
  494.3 3.8 fusion.103
  (377 shorter events, 146.8 us)
Async XLA Ops:
  2.5 10.7 %all-to-all-start = ((bf16[1,32,8,256]{3,1,0,2:T(8,128)(2,1)}), bf16[1,32,8,256]{3,1,0,2:T(8,128)(2,1)S(1)}, u32[]{:S(2)}, u32[]{:S(2)}) async-start(bf16[1,32,8,256]{3,1,0,2:T(8,128)(2,1)} %copy.98), calls=%async_computation | async-start | bytes 262144 | tf_op jit(solution)/shard_map/all_to_all | solution.py:154
  20.3 8.0 %collective-permute-start.3 = (bf16[96,768]{1,0:T(8,128)(2,1)}, bf16[96,768]{1,0:T(8,128)(2,1)}, u32[]{:S(2)}, u32[]{:S(2)}) collective-permute-start(bf16[96,768]{1,0:T(8,128)(2,1)} %get-tuple-element.46), channel_id=1, source_target_pairs={{0,6},{1,7},{2,4},{3,5},{4,2},{5,3},{6,0},{7,1},{8,14},{9,15},{10,... | collective-permute-start | bytes 442376 | tf_op jit(solution)/shard_map/ppermute | solution.py:17
  20.9 9.1 %collective-permute-start.2 = (bf16[96,768]{1,0:T(8,128)(2,1)}, bf16[96,768]{1,0:T(8,128)(2,1)}, u32[]{:S(2)}, u32[]{:S(2)}) collective-permute-start(bf16[96,768]{1,0:T(8,128)(2,1)} %get-tuple-element.47), channel_id=1, source_target_pairs={{0,4},{1,5},{2,6},{3,7},{4,0},{5,1},{6,2},{7,3},{8,12},{9,13},{10,... | collective-permute-start | bytes 442376 | tf_op jit(solution)/shard_map/ppermute | solution.py:17
  22.3 7.6 %collective-permute-start.1 = (bf16[96,768]{1,0:T(8,128)(2,1)}, bf16[96,768]{1,0:T(8,128)(2,1)}, u32[]{:S(2)}, u32[]{:S(2)}) collective-permute-start(bf16[96,768]{1,0:T(8,128)(2,1)} %get-tuple-element.45), channel_id=1, source_target_pairs={{0,2},{1,3},{2,0},{3,1},{4,6},{5,7},{6,4},{7,5},{8,10},{9,11},{10,... | collective-permute-start | bytes 442376 | tf_op jit(solution)/shard_map/ppermute | solution.py:17
  32.4 8.0 %collective-permute-start.5 = (bf16[96,768]{1,0:T(8,128)(2,1)S(1)}, bf16[96,768]{1,0:T(8,128)(2,1)S(1)}, u32[]{:S(2)}, u32[]{:S(2)}) collective-permute-start(bf16[96,768]{1,0:T(8,128)(2,1)S(1)} %fusion.77), channel_id=1, source_target_pairs={{0,4},{1,5},{2,6},{3,7},{4,0},{5,1},{6,2},{7,3},{8,12},{9,13},{10,... | collective-permute-start | bytes 442376 | tf_op jit(solution)/shard_map/ppermute | solution.py:17
  178.0 7.8 %collective-permute-start.8 = (bf16[4,96,768]{2,1,0:T(8,128)(2,1)S(1)}, bf16[4,96,768]{2,1,0:T(8,128)(2,1)S(1)}, u32[]{:S(2)}, u32[]{:S(2)}) collective-permute-start(bf16[4,96,768]{2,1,0:T(8,128)(2,1)S(1)} %fusion.62), channel_id=1, source_target_pairs={{0,1},{1,0},{2,3},{3,2},{4,5},{5,4},{6,7},{7,6},{8,9},{9,8},{10,11... | collective-permute-start | bytes 1769480 | tf_op jit(solution)/shard_map/ppermute | solution.py:17
  186.0 7.7 %collective-permute-start.11 = (bf16[96,768]{1,0:T(8,128)(2,1)S(1)}, bf16[96,768]{1,0:T(8,128)(2,1)S(1)}, u32[]{:S(2)}, u32[]{:S(2)}) collective-permute-start(bf16[96,768]{1,0:T(8,128)(2,1)S(1)} %get-tuple-element.43), channel_id=1, source_target_pairs={{0,6},{1,7},{2,4},{3,5},{4,2},{5,3},{6,0},{7,1},{8,14},{9,15},{10,... | collective-permute-start | bytes 442376 | tf_op jit(solution)/shard_map/ppermute | solution.py:17
  187.5 8.4 %collective-permute-start.10 = (bf16[96,768]{1,0:T(8,128)(2,1)S(1)}, bf16[96,768]{1,0:T(8,128)(2,1)S(1)}, u32[]{:S(2)}, u32[]{:S(2)}) collective-permute-start(bf16[96,768]{1,0:T(8,128)(2,1)S(1)} %get-tuple-element.44), channel_id=1, source_target_pairs={{0,4},{1,5},{2,6},{3,7},{4,0},{5,1},{6,2},{7,3},{8,12},{9,13},{10,... | collective-permute-start | bytes 442376 | tf_op jit(solution)/shard_map/ppermute | solution.py:17
  196.0 7.7 %collective-permute-start.14 = (bf16[96,768]{1,0:T(8,128)(2,1)S(1)}, bf16[96,768]{1,0:T(8,128)(2,1)S(1)}, u32[]{:S(2)}, u32[]{:S(2)}) collective-permute-start(bf16[96,768]{1,0:T(8,128)(2,1)S(1)} %fusion.74), channel_id=1, source_target_pairs={{0,6},{1,7},{2,4},{3,5},{4,2},{5,3},{6,0},{7,1},{8,14},{9,15},{10,... | collective-permute-start | bytes 442376 | tf_op jit(solution)/shard_map/ppermute | solution.py:17
  197.5 8.4 %collective-permute-start.13 = (bf16[96,768]{1,0:T(8,128)(2,1)S(1)}, bf16[96,768]{1,0:T(8,128)(2,1)S(1)}, u32[]{:S(2)}, u32[]{:S(2)}) collective-permute-start(bf16[96,768]{1,0:T(8,128)(2,1)S(1)} %fusion.74), channel_id=1, source_target_pairs={{0,4},{1,5},{2,6},{3,7},{4,0},{5,1},{6,2},{7,3},{8,12},{9,13},{10,... | collective-permute-start | bytes 442376 | tf_op jit(solution)/shard_map/ppermute | solution.py:17
  201.1 33.0 %collective-permute-start.21 = (bf16[1536,768]{1,0:T(8,128)(2,1)}, bf16[1536,768]{1,0:T(8,128)(2,1)}, u32[]{:S(2)}, u32[]{:S(2)}) collective-permute-start(bf16[1536,768]{1,0:T(8,128)(2,1)} %dynamic-slice_bitcast_fusion.2), channel_id=1, source_target_pairs={{0,1},{1,0},{2,3},{3,2},{4,5},{5,4},{6,7},{7,6},{8,9},{9,8},{10,11... | collective-permute-start | bytes 7077896 | tf_op jit(solution)/shard_map/ppermute | solution.py:17
  217.3 23.2 %collective-permute-start.35 = (bf16[384,3072]{1,0:T(8,128)(2,1)}, bf16[384,3072]{1,0:T(8,128)(2,1)}, u32[]{:S(2)}, u32[]{:S(2)}) collective-permute-start(bf16[384,3072]{1,0:T(8,128)(2,1)} %dynamic-slice_bitcast_fusion.1), channel_id=1, source_target_pairs={{0,1},{1,0},{2,3},{3,2},{4,5},{5,4},{6,7},{7,6},{8,9},{9,8},{10,11... | collective-permute-start | bytes 7077896 | tf_op jit(solution)/shard_map/ppermute | solution.py:17
  220.4 22.9 %collective-permute-start.47 = (bf16[1536,768]{1,0:T(8,128)(2,1)}, bf16[1536,768]{1,0:T(8,128)(2,1)}, u32[]{:S(2)}, u32[]{:S(2)}) collective-permute-start(bf16[1536,768]{1,0:T(8,128)(2,1)} %dynamic-slice_bitcast_fusion), channel_id=1, source_target_pairs={{0,1},{1,0},{2,3},{3,2},{4,5},{5,4},{6,7},{7,6},{8,9},{9,8},{10,11... | collective-permute-start | bytes 7077896 | tf_op jit(solution)/shard_map/ppermute | solution.py:17
  227.1 218.1 %all-to-all-start.1 = ((bf16[8,32,1,256]{3,1,2,0:T(8,128)(2,1)}), bf16[8,32,1,256]{3,1,2,0:T(8,128)(2,1)}, u32[]{:S(2)}, u32[]{:S(2)}) async-start(bf16[8,32,1,256]{3,1,2,0:T(8,128)(2,1)} %bitcast.88), calls=%async_computation.1 | async-start | bytes 262144 | tf_op jit(solution)/shard_map/all_to_all | solution.py:214
  231.4 214.7 %collective-permute-start.20 = (f32[4,768]{1,0:T(4,128)S(1)}, f32[4,768]{1,0:T(4,128)}, u32[]{:S(2)}, u32[]{:S(2)}) collective-permute-start(f32[4,768]{1,0:T(4,128)S(1)} %add.294), channel_id=1, source_target_pairs={{0,16},{8,24},{16,0},{24,8},{1,17},{9,25},{17,1},{25,9},{2,18},{10... | collective-permute-start | bytes 36872 | tf_op jit(solution)/shard_map/ppermute | solution.py:17
  236.9 16.2 %collective-permute-start.24 = (bf16[384,768]{1,0:T(8,128)(2,1)S(1)}, bf16[384,768]{1,0:T(8,128)(2,1)S(1)}, u32[]{:S(2)}, u32[]{:S(2)}) collective-permute-start(bf16[384,768]{1,0:T(8,128)(2,1)S(1)} %dynamic-slice_bitcast_fusion.7), channel_id=1, source_target_pairs={{0,4},{1,5},{2,6},{3,7},{4,0},{5,1},{6,2},{7,3},{8,12},{9,13},{10,... | collective-permute-start | bytes 1769480 | tf_op jit(solution)/shard_map/ppermute | solution.py:17
  239.0 28.8 %collective-permute-start.22 = (bf16[384,768]{1,0:T(8,128)(2,1)S(1)}, bf16[384,768]{1,0:T(8,128)(2,1)S(1)}, u32[]{:S(2)}, u32[]{:S(2)}) collective-permute-start(bf16[384,768]{1,0:T(8,128)(2,1)S(1)} %dynamic-slice_bitcast_fusion.8), channel_id=1, source_target_pairs={{0,2},{1,3},{2,0},{3,1},{4,6},{5,7},{6,4},{7,5},{8,10},{9,11},{10,... | collective-permute-start | bytes 1769480 | tf_op jit(solution)/shard_map/ppermute | solution.py:17
  242.7 23.1 %collective-permute-start.38 = (bf16[96,3072]{1,0:T(8,128)(2,1)S(1)}, bf16[96,3072]{1,0:T(8,128)(2,1)S(1)}, u32[]{:S(2)}, u32[]{:S(2)}) collective-permute-start(bf16[96,3072]{1,0:T(8,128)(2,1)S(1)} %dynamic-slice_bitcast_fusion.5), channel_id=1, source_target_pairs={{0,4},{1,5},{2,6},{3,7},{4,0},{5,1},{6,2},{7,3},{8,12},{9,13},{10,... | collective-permute-start | bytes 1769480 | tf_op jit(solution)/shard_map/ppermute | solution.py:17
  243.4 24.7 %collective-permute-start.36 = (bf16[96,3072]{1,0:T(8,128)(2,1)S(1)}, bf16[96,3072]{1,0:T(8,128)(2,1)S(1)}, u32[]{:S(2)}, u32[]{:S(2)}) collective-permute-start(bf16[96,3072]{1,0:T(8,128)(2,1)S(1)} %dynamic-slice_bitcast_fusion.6), channel_id=1, source_target_pairs={{0,2},{1,3},{2,0},{3,1},{4,6},{5,7},{6,4},{7,5},{8,10},{9,11},{10,... | collective-permute-start | bytes 1769480 | tf_op jit(solution)/shard_map/ppermute | solution.py:17
  253.2 25.3 %collective-permute-start.50 = (bf16[384,768]{1,0:T(8,128)(2,1)S(1)}, bf16[384,768]{1,0:T(8,128)(2,1)S(1)}, u32[]{:S(2)}, u32[]{:S(2)}) collective-permute-start(bf16[384,768]{1,0:T(8,128)(2,1)S(1)} %dynamic-slice_bitcast_fusion.3), channel_id=1, source_target_pairs={{0,4},{1,5},{2,6},{3,7},{4,0},{5,1},{6,2},{7,3},{8,12},{9,13},{10,... | collective-permute-start | bytes 1769480 | tf_op jit(solution)/shard_map/ppermute | solution.py:17
  265.8 16.3 %collective-permute-start.48 = (bf16[384,768]{1,0:T(8,128)(2,1)S(1)}, bf16[384,768]{1,0:T(8,128)(2,1)S(1)}, u32[]{:S(2)}, u32[]{:S(2)}) collective-permute-start(bf16[384,768]{1,0:T(8,128)(2,1)S(1)} %dynamic-slice_bitcast_fusion.4), channel_id=1, source_target_pairs={{0,2},{1,3},{2,0},{3,1},{4,6},{5,7},{6,4},{7,5},{8,10},{9,11},{10,... | collective-permute-start | bytes 1769480 | tf_op jit(solution)/shard_map/ppermute | solution.py:17
  267.9 20.5 %collective-permute-start.25 = (bf16[192,768]{1,0:T(8,128)(2,1)S(1)}, bf16[192,768]{1,0:T(8,128)(2,1)S(1)}, u32[]{:S(2)}, u32[]{:S(2)}) collective-permute-start(bf16[192,768]{1,0:T(8,128)(2,1)S(1)} %dynamic-slice_bitcast_fusion.13), channel_id=1, source_target_pairs={{0,2},{1,3},{2,0},{3,1},{4,6},{5,7},{6,4},{7,5},{8,10},{9,11},{10,... | collective-permute-start | bytes 884744 | tf_op jit(solution)/shard_map/ppermute | solution.py:17
  268.1 22.3 %collective-permute-start.23 = (bf16[192,768]{1,0:T(8,128)(2,1)S(1)}, bf16[192,768]{1,0:T(8,128)(2,1)S(1)}, u32[]{:S(2)}, u32[]{:S(2)}) collective-permute-start(bf16[192,768]{1,0:T(8,128)(2,1)S(1)} %dynamic-slice_bitcast_fusion.14), channel_id=1, source_target_pairs={{0,4},{1,5},{2,6},{3,7},{4,0},{5,1},{6,2},{7,3},{8,12},{9,13},{10,... | collective-permute-start | bytes 884744 | tf_op jit(solution)/shard_map/ppermute | solution.py:17
  278.4 16.3 %collective-permute-start.39 = (bf16[48,3072]{1,0:T(8,128)(2,1)S(1)}, bf16[48,3072]{1,0:T(8,128)(2,1)S(1)}, u32[]{:S(2)}, u32[]{:S(2)}) collective-permute-start(bf16[48,3072]{1,0:T(8,128)(2,1)S(1)} %dynamic-slice_bitcast_fusion.11), channel_id=1, source_target_pairs={{0,2},{1,3},{2,0},{3,1},{4,6},{5,7},{6,4},{7,5},{8,10},{9,11},{10,... | collective-permute-start | bytes 884744 | tf_op jit(solution)/shard_map/ppermute | solution.py:17
  282.1 13.1 %collective-permute-start.37 = (bf16[48,3072]{1,0:T(8,128)(2,1)S(1)}, bf16[48,3072]{1,0:T(8,128)(2,1)S(1)}, u32[]{:S(2)}, u32[]{:S(2)}) collective-permute-start(bf16[48,3072]{1,0:T(8,128)(2,1)S(1)} %dynamic-slice_bitcast_fusion.12), channel_id=1, source_target_pairs={{0,4},{1,5},{2,6},{3,7},{4,0},{5,1},{6,2},{7,3},{8,12},{9,13},{10,... | collective-permute-start | bytes 884744 | tf_op jit(solution)/shard_map/ppermute | solution.py:17
  288.4 10.2 %collective-permute-start.51 = (bf16[192,768]{1,0:T(8,128)(2,1)S(1)}, bf16[192,768]{1,0:T(8,128)(2,1)S(1)}, u32[]{:S(2)}, u32[]{:S(2)}) collective-permute-start(bf16[192,768]{1,0:T(8,128)(2,1)S(1)} %dynamic-slice_bitcast_fusion.9), channel_id=1, source_target_pairs={{0,2},{1,3},{2,0},{3,1},{4,6},{5,7},{6,4},{7,5},{8,10},{9,11},{10,... | collective-permute-start | bytes 884744 | tf_op jit(solution)/shard_map/ppermute | solution.py:17
  290.4 8.2 %collective-permute-start.49 = (bf16[192,768]{1,0:T(8,128)(2,1)S(1)}, bf16[192,768]{1,0:T(8,128)(2,1)S(1)}, u32[]{:S(2)}, u32[]{:S(2)}) collective-permute-start(bf16[192,768]{1,0:T(8,128)(2,1)S(1)} %dynamic-slice_bitcast_fusion.10), channel_id=1, source_target_pairs={{0,4},{1,5},{2,6},{3,7},{4,0},{5,1},{6,2},{7,3},{8,12},{9,13},{10,... | collective-permute-start | bytes 884744 | tf_op jit(solution)/shard_map/ppermute | solution.py:17
  294.7 22.6 %collective-permute-start.26 = (bf16[2,192,768]{2,1,0:T(8,128)(2,1)S(1)}, bf16[2,192,768]{2,1,0:T(8,128)(2,1)S(1)}, u32[]{:S(2)}, u32[]{:S(2)}) collective-permute-start(bf16[2,192,768]{2,1,0:T(8,128)(2,1)S(1)} %pad_maximum_fusion.8), channel_id=1, source_target_pairs={{0,8},{8,0},{16,24},{24,16},{1,9},{9,1},{17,25},{25,17},{2,10},{10... | collective-permute-start | bytes 1769480 | tf_op jit(solution)/shard_map/ppermute | solution.py:17
  295.3 42.8 %collective-permute-start.40 = (bf16[2,48,3072]{2,1,0:T(8,128)(2,1)S(1)}, bf16[2,48,3072]{2,1,0:T(8,128)(2,1)S(1)}, u32[]{:S(2)}, u32[]{:S(2)}) collective-permute-start(bf16[2,48,3072]{2,1,0:T(8,128)(2,1)S(1)} %pad_maximum_fusion.9), channel_id=1, source_target_pairs={{0,8},{8,0},{16,24},{24,16},{1,9},{9,1},{17,25},{25,17},{2,10},{10... | collective-permute-start | bytes 1769480 | tf_op jit(solution)/shard_map/ppermute | solution.py:17
  298.7 46.2 %collective-permute-start.52 = (bf16[2,192,768]{2,1,0:T(8,128)(2,1)S(1)}, bf16[2,192,768]{2,1,0:T(8,128)(2,1)S(1)}, u32[]{:S(2)}, u32[]{:S(2)}) collective-permute-start(bf16[2,192,768]{2,1,0:T(8,128)(2,1)S(1)} %pad_maximum_fusion.10), channel_id=1, source_target_pairs={{0,8},{8,0},{16,24},{24,16},{1,9},{9,1},{17,25},{25,17},{2,10},{10... | collective-permute-start | bytes 1769480 | tf_op jit(solution)/shard_map/ppermute | solution.py:17
  317.4 55.1 %collective-permute-start.27 = (bf16[2,192,768]{2,1,0:T(8,128)(2,1)S(1)}, bf16[2,192,768]{2,1,0:T(8,128)(2,1)S(1)}, u32[]{:S(2)}, u32[]{:S(2)}) collective-permute-start(bf16[2,192,768]{2,1,0:T(8,128)(2,1)S(1)} %fusion.94), channel_id=1, source_target_pairs={{0,16},{8,24},{16,0},{24,8},{1,17},{9,25},{17,1},{25,9},{2,18},{10... | collective-permute-start | bytes 1769480 | tf_op jit(solution)/shard_map/ppermute | solution.py:17
  338.2 46.9 %collective-permute-start.41 = (bf16[2,48,3072]{2,1,0:T(8,128)(2,1)S(1)}, bf16[2,48,3072]{2,1,0:T(8,128)(2,1)S(1)}, u32[]{:S(2)}, u32[]{:S(2)}) collective-permute-start(bf16[2,48,3072]{2,1,0:T(8,128)(2,1)S(1)} %fusion.93), channel_id=1, source_target_pairs={{0,16},{8,24},{16,0},{24,8},{1,17},{9,25},{17,1},{25,9},{2,18},{10... | collective-permute-start | bytes 1769480 | tf_op jit(solution)/shard_map/ppermute | solution.py:17
  345.0 46.5 %collective-permute-start.53 = (bf16[2,192,768]{2,1,0:T(8,128)(2,1)S(1)}, bf16[2,192,768]{2,1,0:T(8,128)(2,1)S(1)}, u32[]{:S(2)}, u32[]{:S(2)}) collective-permute-start(bf16[2,192,768]{2,1,0:T(8,128)(2,1)S(1)} %fusion.92), channel_id=1, source_target_pairs={{0,16},{8,24},{16,0},{24,8},{1,17},{9,25},{17,1},{25,9},{2,18},{10... | collective-permute-start | bytes 1769480 | tf_op jit(solution)/shard_map/ppermute | solution.py:17
  372.7 32.3 %collective-permute-start.30 = (bf16[192,768]{1,0:T(8,128)(2,1)S(1)}, bf16[192,768]{1,0:T(8,128)(2,1)S(1)}, u32[]{:S(2)}, u32[]{:S(2)}) collective-permute-start(bf16[192,768]{1,0:T(8,128)(2,1)S(1)} %get-tuple-element.58), channel_id=1, source_target_pairs={{0,2},{1,3},{2,0},{3,1},{4,6},{5,7},{6,4},{7,5},{8,10},{9,11},{10,... | collective-permute-start | bytes 884744 | tf_op jit(solution)/shard_map/ppermute | solution.py:17
  385.3 9.1 %collective-permute-start.44 = (bf16[48,3072]{1,0:T(8,128)(2,1)S(1)}, bf16[48,3072]{1,0:T(8,128)(2,1)S(1)}, u32[]{:S(2)}, u32[]{:S(2)}) collective-permute-start(bf16[48,3072]{1,0:T(8,128)(2,1)S(1)} %get-tuple-element.54), channel_id=1, source_target_pairs={{0,2},{1,3},{2,0},{3,1},{4,6},{5,7},{6,4},{7,5},{8,10},{9,11},{10,... | collective-permute-start | bytes 884744 | tf_op jit(solution)/shard_map/ppermute | solution.py:17
  385.4 19.1 %collective-permute-start.42 = (bf16[48,3072]{1,0:T(8,128)(2,1)S(1)}, bf16[48,3072]{1,0:T(8,128)(2,1)S(1)}, u32[]{:S(2)}, u32[]{:S(2)}) collective-permute-start(bf16[48,3072]{1,0:T(8,128)(2,1)S(1)} %get-tuple-element.53), channel_id=1, source_target_pairs={{0,4},{1,5},{2,6},{3,7},{4,0},{5,1},{6,2},{7,3},{8,12},{9,13},{10,... | collective-permute-start | bytes 884744 | tf_op jit(solution)/shard_map/ppermute | solution.py:17
  394.4 9.9 %collective-permute-start.54 = (bf16[192,768]{1,0:T(8,128)(2,1)S(1)}, bf16[192,768]{1,0:T(8,128)(2,1)S(1)}, u32[]{:S(2)}, u32[]{:S(2)}) collective-permute-start(bf16[192,768]{1,0:T(8,128)(2,1)S(1)} %get-tuple-element.49), channel_id=1, source_target_pairs={{0,4},{1,5},{2,6},{3,7},{4,0},{5,1},{6,2},{7,3},{8,12},{9,13},{10,... | collective-permute-start | bytes 884744 | tf_op jit(solution)/shard_map/ppermute | solution.py:17
  398.7 33.3 %collective-permute-start.45 = (bf16[96,3072]{1,0:T(8,128)(2,1)S(1)}, bf16[96,3072]{1,0:T(8,128)(2,1)S(1)}, u32[]{:S(2)}, u32[]{:S(2)}) collective-permute-start(bf16[96,3072]{1,0:T(8,128)(2,1)S(1)} %bitcast.388), channel_id=1, source_target_pairs={{0,4},{1,5},{2,6},{3,7},{4,0},{5,1},{6,2},{7,3},{8,12},{9,13},{10,... | collective-permute-start | bytes 1769480 | tf_op jit(solution)/shard_map/ppermute | solution.py:17
  404.4 25.3 %collective-permute-start.57 = (bf16[384,768]{1,0:T(8,128)(2,1)S(1)}, bf16[384,768]{1,0:T(8,128)(2,1)S(1)}, u32[]{:S(2)}, u32[]{:S(2)}) collective-permute-start(bf16[384,768]{1,0:T(8,128)(2,1)S(1)} %bitcast.394), channel_id=1, source_target_pairs={{0,4},{1,5},{2,6},{3,7},{4,0},{5,1},{6,2},{7,3},{8,12},{9,13},{10,... | collective-permute-start | bytes 1769480 | tf_op jit(solution)/shard_map/ppermute | solution.py:17
  404.5 25.4 %collective-permute-start.55 = (bf16[384,768]{1,0:T(8,128)(2,1)S(1)}, bf16[384,768]{1,0:T(8,128)(2,1)S(1)}, u32[]{:S(2)}, u32[]{:S(2)}) collective-permute-start(bf16[384,768]{1,0:T(8,128)(2,1)S(1)} %bitcast.396), channel_id=1, source_target_pairs={{0,2},{1,3},{2,0},{3,1},{4,6},{5,7},{6,4},{7,5},{8,10},{9,11},{10,... | collective-permute-start | bytes 1769480 | tf_op jit(solution)/shard_map/ppermute | solution.py:17
  404.9 36.8 %collective-permute-start.28 = (bf16[192,768]{1,0:T(8,128)(2,1)S(1)}, bf16[192,768]{1,0:T(8,128)(2,1)S(1)}, u32[]{:S(2)}, u32[]{:S(2)}) collective-permute-start(bf16[192,768]{1,0:T(8,128)(2,1)S(1)} %get-tuple-element.57), channel_id=1, source_target_pairs={{0,4},{1,5},{2,6},{3,7},{4,0},{5,1},{6,2},{7,3},{8,12},{9,13},{10,... | collective-permute-start | bytes 884744 | tf_op jit(solution)/shard_map/ppermute | solution.py:17
  429.6 21.7 %collective-permute-start.31 = (bf16[384,768]{1,0:T(8,128)(2,1)S(1)}, bf16[384,768]{1,0:T(8,128)(2,1)}, u32[]{:S(2)}, u32[]{:S(2)}) collective-permute-start(bf16[384,768]{1,0:T(8,128)(2,1)S(1)} %bitcast.386), channel_id=1, source_target_pairs={{0,4},{1,5},{2,6},{3,7},{4,0},{5,1},{6,2},{7,3},{8,12},{9,13},{10,... | collective-permute-start | bytes 1769480 | tf_op jit(solution)/shard_map/ppermute | solution.py:17
  429.9 9.9 %collective-permute-start.43 = (bf16[96,3072]{1,0:T(8,128)(2,1)S(1)}, bf16[96,3072]{1,0:T(8,128)(2,1)S(1)}, u32[]{:S(2)}, u32[]{:S(2)}) collective-permute-start(bf16[96,3072]{1,0:T(8,128)(2,1)S(1)} %bitcast.392), channel_id=1, source_target_pairs={{0,2},{1,3},{2,0},{3,1},{4,6},{5,7},{6,4},{7,5},{8,10},{9,11},{10,... | collective-permute-start | bytes 1769480 | tf_op jit(solution)/shard_map/ppermute | solution.py:17
  432.0 28.2 %collective-permute-start.58 = (bf16[1536,768]{1,0:T(8,128)(2,1)}, bf16[1536,768]{1,0:T(8,128)(2,1)}, u32[]{:S(2)}, u32[]{:S(2)}) collective-permute-start(bf16[1536,768]{1,0:T(8,128)(2,1)} %bitcast.156), channel_id=1, source_target_pairs={{0,1},{1,0},{2,3},{3,2},{4,5},{5,4},{6,7},{7,6},{8,9},{9,8},{10,11... | collective-permute-start | bytes 7077896 | tf_op jit(solution)/shard_map/ppermute | solution.py:17
  441.7 25.3 %collective-permute-start.46 = (bf16[384,3072]{1,0:T(8,128)(2,1)}, bf16[384,3072]{1,0:T(8,128)(2,1)}, u32[]{:S(2)}, u32[]{:S(2)}) collective-permute-start(bf16[384,3072]{1,0:T(8,128)(2,1)} %bitcast.122), channel_id=1, source_target_pairs={{0,1},{1,0},{2,3},{3,2},{4,5},{5,4},{6,7},{7,6},{8,9},{9,8},{10,11... | collective-permute-start | bytes 7077896 | tf_op jit(solution)/shard_map/ppermute | solution.py:17
  441.8 15.9 %collective-permute-start.29 = (bf16[384,768]{1,0:T(8,128)(2,1)S(1)}, bf16[384,768]{1,0:T(8,128)(2,1)}, u32[]{:S(2)}, u32[]{:S(2)}) collective-permute-start(bf16[384,768]{1,0:T(8,128)(2,1)S(1)} %bitcast.390), channel_id=1, source_target_pairs={{0,2},{1,3},{2,0},{3,1},{4,6},{5,7},{6,4},{7,5},{8,10},{9,11},{10,... | collective-permute-start | bytes 1769480 | tf_op jit(solution)/shard_map/ppermute | solution.py:17
  451.3 8.2 %collective-permute-start.34 = (bf16[32,2048]{1,0:T(8,128)(2,1)S(1)}, bf16[32,2048]{1,0:T(8,128)(2,1)S(1)}, u32[]{:S(2)}, u32[]{:S(2)}) collective-permute-start(bf16[32,2048]{1,0:T(8,128)(2,1)S(1)} %add.307), channel_id=1, source_target_pairs={{0,16},{8,24},{16,0},{24,8},{1,17},{9,25},{17,1},{25,9},{2,18},{10... | collective-permute-start | bytes 393224 | tf_op jit(solution)/shard_map/ppermute | solution.py:17
  459.4 30.9 %collective-permute-start.32 = (bf16[1536,768]{1,0:T(8,128)(2,1)S(1)}, bf16[1536,768]{1,0:T(8,128)(2,1)S(1)}, u32[]{:S(2)}, u32[]{:S(2)}) collective-permute-start(bf16[1536,768]{1,0:T(8,128)(2,1)S(1)} %bitcast.335), channel_id=1, source_target_pairs={{0,1},{1,0},{2,3},{3,2},{4,5},{5,4},{6,7},{7,6},{8,9},{9,8},{10,11... | collective-permute-start | bytes 7077896 | tf_op jit(solution)/shard_map/ppermute | solution.py:17
  (84 other events, 818.9 us)
